TPU v7x, 256 devices: a whole 4x4x8 slice. The times are simulated.
256 devices in a mesh: dp: 8 (over x, core), graph: 32 (over z, y).
Axes of the slice: x: 4, y: 4, z: 8, core: 2. Of those that a mesh axis runs over, the one named last changes fastest.
Arguments:
- feats: bfloat16 [8, 16384, 512], P('dp', 'graph'), may hold values from -6 to 6
- grad_out: bfloat16 [8, 16384, 512], P('dp', 'graph'), may hold values from -6 to 6
- w_self: bfloat16 [512, 512], replicated, may hold values from -0.25 to 0.25
- w_neigh: bfloat16 [512, 512], replicated, may hold values from -0.25 to 0.25
- nbr: int32 [8, 16384, 10], P('dp', 'graph'), may hold values from 0 to 2047, as said below
- deg: int32 [8, 16384], P('dp', 'graph'), may hold values from 1 to 10
- hub_rows: int32 [8, 512], P('dp', 'graph'), may hold values from 0 to 511, as said below
- send_rows: int32 [8, 32, 32, 32], P('dp', 'graph'), may hold values from 0 to 511
Outputs:
- out: bfloat16 [8, 16384, 512], P('dp', 'graph')
- grad_feats: bfloat16 [8, 16384, 512], P('dp', 'graph')
- grad_w_self: float32 [512, 512], P('graph')
- grad_w_neigh: float32 [512, 512], P('graph')
Inputs may be any that keep to these rules, and one draw needn't show every extreme that they name: `hub_rows`: within each partition's block of 16 entries the rows are distinct rows of that partition. `nbr`: entries name rows of the partition's table: below 512 its own rows, then 512 hub rows, then 1024 received rows. Only slots below deg are live.
All inputs are finite; a program needn't handle non-finite values.
Results may differ from a plain program's by a relative error of at most 0.007.
Values may be sent and summed in bfloat16 or wider, within the bound.
A program may use at most 64 MiB of HBM per device.

v0:
```python
import jax
import jax.numpy as jnp
from jax import lax
from jax.sharding import PartitionSpec as P


def shards(feats, grad_out, w_self, w_neigh, nbr, deg, hub_rows, send_rows):
    own = feats[0]
    grads = grad_out[0]
    rows, width = own.shape
    idx = nbr[0]
    dcount = deg[0]
    hub_idx = hub_rows[0]
    sent_idx = send_rows[0, 0]
    hub_local = own[hub_idx]
    hubs = lax.all_gather(hub_local, "graph", axis=0, tiled=True)
    outgoing = own[sent_idx]
    incoming = lax.all_to_all(outgoing, "graph", split_axis=0, concat_axis=0, tiled=True)
    nhub = hubs.shape[0]
    table = jnp.concatenate([own, hubs, incoming.reshape(-1, width)], axis=0)
    slots = idx.shape[1]
    live = jnp.arange(slots)[None, :] < dcount[:, None]
    total = jnp.zeros((rows, width), jnp.float32)
    for k in range(slots):
        total = total + jnp.where(live[:, k : k + 1], table[idx[:, k]].astype(jnp.float32), 0.0)
    degree = dcount.astype(jnp.float32)[:, None]
    agg = (total / degree).astype(jnp.bfloat16)
    result = (
        jnp.dot(own, w_self, preferred_element_type=jnp.float32)
        + jnp.dot(agg, w_neigh, preferred_element_type=jnp.float32)
    ).astype(jnp.bfloat16)
    trans = (((1,), (1,)), ((), ()))
    back = lax.dot_general(grads, w_neigh, trans, preferred_element_type=jnp.float32) / degree
    height = table.shape[0]
    dtable = jnp.zeros((height, width), jnp.float32)
    for k in range(slots):
        target = jnp.where(live[:, k], idx[:, k], height)
        dtable = dtable.at[target].add(back, mode="drop")
    hub_back = lax.psum_scatter(
        dtable[rows : rows + nhub].astype(jnp.bfloat16), "graph", scatter_dimension=0, tiled=True
    ).astype(jnp.float32)
    recv_back = lax.all_to_all(
        dtable[rows + nhub :].reshape(incoming.shape).astype(jnp.bfloat16),
        "graph",
        split_axis=0,
        concat_axis=0,
        tiled=True,
    ).astype(jnp.float32)
    inner = (((0,), (0,)), ((), ()))
    dws = lax.dot_general(own, grads, inner, preferred_element_type=jnp.float32)
    dwn = lax.dot_general(agg, grads, inner, preferred_element_type=jnp.float32)
    dlocal = (
        lax.dot_general(grads, w_self, trans, preferred_element_type=jnp.float32) + dtable[:rows]
    )
    dlocal = dlocal.at[hub_idx].add(hub_back)
    dlocal = dlocal.at[sent_idx.reshape(-1)].add(recv_back.reshape(-1, width))
    grad_rows = dlocal.astype(jnp.bfloat16)
    share = width // lax.axis_size("graph")
    sum_self, sum_neigh = lax.psum((dws, dwn), ("dp", "graph"))
    start = lax.axis_index("graph") * share
    sum_self = lax.dynamic_slice_in_dim(sum_self, start, share, 0)
    sum_neigh = lax.dynamic_slice_in_dim(sum_neigh, start, share, 0)
    count = lax.axis_size("dp") * lax.axis_size("graph") * rows
    scale = 1.0 / jnp.sqrt(jnp.float32(count))
    return (result[None], grad_rows[None], sum_self * scale, sum_neigh * scale)


def solution(mesh):
    placed = (
        P("dp", "graph", None),
        P("dp", "graph", None),
        P(),
        P(),
        P("dp", "graph", None),
        P("dp", "graph"),
        P("dp", "graph"),
        P("dp", "graph", None, None),
    )
    return jax.shard_map(
        shards,
        mesh=mesh,
        in_specs=placed,
        out_specs=(
            P("dp", "graph", None),
            P("dp", "graph", None),
            P("graph", None),
            P("graph", None),
        ),
        check_vma=False,
    )
```

profile of v0, /device:TPU:2, one launch (start us, length us, event | category | flops | bytes accessed | tf_op | source)
XLA Modules:
  0.0 481.6 jit_solution(7234979474906921619)
XLA Ops:
  8.0 0.8 compare_select_fusion
  8.8 0.1 reshape.124
  8.9 6.3 %gather_fusion.1 = bf16[1024,512]{1,0:T(8,128)(2,1)} fusion(bf16[512,512]{1,0:T(8,128)(2,1)} %bitcast.64, s32[1024]{0:T(1024)S(1)} %broadcast_clamp_fusion), kind=kCustom, calls=%fused_computation.1 | custom fusion | bytes 2101248 | tf_op jit(solution)/shard_map/gather | solution.py:17
  15.2 11.6 %all-to-all-start = ((bf16[32,32,512]{2,1,0:T(8,128)(2,1)}), bf16[32,32,512]{2,1,0:T(8,128)(2,1)}, u32[]{:S(2)}, u32[]{:S(2)}) async-start(bf16[32,32,512]{2,1,0:T(8,128)(2,1)} %bitcast.5), calls=%async_computation | async-start | bytes 2097152 | tf_op jit(solution)/shard_map/all_to_all | solution.py:18
  26.8 0.0 reduce-scatter.2.cloned.1.call-start
  27.0 0.5 convolution_divide_fusion
  27.5 5.7 %scatter_custom_fusion = f32[2048,512]{1,0:T(8,128)} fusion(s32[512]{0:T(512)S(1)} %bitcast.92, f32[512,512]{1,0:T(8,128)S(1)} %convolution_divide_fusion, f32[]{:T(128)} %constant.10.clone.1), kind=kCustom, calls=%fused_computation.27 | custom fusion | flops 262144 | bytes 4194308 | tf_op jit(solution)/shard_map/scatter-add | solution.py:38
  33.2 7.6 %scatter_fusion = f32[2048,512]{1,0:T(8,128)} fusion(f32[2048,512]{1,0:T(8,128)} %scatter_custom_fusion, s32[512]{0:T(512)S(1)} %bitcast.77, f32[512,512]{1,0:T(8,128)S(1)} %convolution_divide_fusion), kind=kCustom, calls=%fused_computation.13 | custom fusion | flops 262144 | bytes 3147776 | tf_op jit(solution)/shard_map/scatter-add | solution.py:38
  40.8 8.1 %scatter_fusion.1 = f32[2048,512]{1,0:T(8,128)} fusion(f32[2048,512]{1,0:T(8,128)} %scatter_fusion, s32[512]{0:T(512)S(1)} %bitcast.76, f32[512,512]{1,0:T(8,128)S(1)} %convolution_divide_fusion), kind=kCustom, calls=%fused_computation.14 | custom fusion | flops 262144 | bytes 3147776 | tf_op jit(solution)/shard_map/scatter-add | solution.py:38
  49.0 7.6 %scatter_fusion.2 = f32[2048,512]{1,0:T(8,128)} fusion(f32[2048,512]{1,0:T(8,128)} %scatter_fusion.1, s32[512]{0:T(512)S(1)} %bitcast.75, f32[512,512]{1,0:T(8,128)S(1)} %convolution_divide_fusion), kind=kCustom, calls=%fused_computation.15 | custom fusion | flops 262144 | bytes 3147776 | tf_op jit(solution)/shard_map/scatter-add | solution.py:38
  56.6 7.6 %scatter_fusion.3 = f32[2048,512]{1,0:T(8,128)} fusion(f32[2048,512]{1,0:T(8,128)} %scatter_fusion.2, s32[512]{0:T(512)S(1)} %bitcast.74, f32[512,512]{1,0:T(8,128)S(1)} %convolution_divide_fusion), kind=kCustom, calls=%fused_computation.16 | custom fusion | flops 262144 | bytes 3147776 | tf_op jit(solution)/shard_map/scatter-add | solution.py:38
  64.3 7.6 %scatter_fusion.4 = f32[2048,512]{1,0:T(8,128)} fusion(f32[2048,512]{1,0:T(8,128)} %scatter_fusion.3, s32[512]{0:T(512)S(1)} %bitcast.73, f32[512,512]{1,0:T(8,128)S(1)} %convolution_divide_fusion), kind=kCustom, calls=%fused_computation.17 | custom fusion | flops 262144 | bytes 3147776 | tf_op jit(solution)/shard_map/scatter-add | solution.py:38
  71.9 7.8 %scatter_fusion.5 = f32[2048,512]{1,0:T(8,128)} fusion(f32[2048,512]{1,0:T(8,128)} %scatter_fusion.4, s32[512]{0:T(512)S(1)} %bitcast.72, f32[512,512]{1,0:T(8,128)S(1)} %convolution_divide_fusion), kind=kCustom, calls=%fused_computation.18 | custom fusion | flops 262144 | bytes 3147776 | tf_op jit(solution)/shard_map/scatter-add | solution.py:38
  79.7 7.6 %scatter_fusion.6 = f32[2048,512]{1,0:T(8,128)} fusion(f32[2048,512]{1,0:T(8,128)} %scatter_fusion.5, s32[512]{0:T(512)S(1)} %bitcast.71, f32[512,512]{1,0:T(8,128)S(1)} %convolution_divide_fusion), kind=kCustom, calls=%fused_computation.19 | custom fusion | flops 262144 | bytes 3147776 | tf_op jit(solution)/shard_map/scatter-add | solution.py:38
  87.4 7.6 %scatter_fusion.7 = f32[2048,512]{1,0:T(8,128)} fusion(f32[2048,512]{1,0:T(8,128)} %scatter_fusion.6, s32[512]{0:T(512)S(1)} %bitcast.78, f32[512,512]{1,0:T(8,128)S(1)} %convolution_divide_fusion), kind=kCustom, calls=%fused_computation.20 | custom fusion | flops 262144 | bytes 3147776 | tf_op jit(solution)/shard_map/scatter-add | solution.py:38
  95.0 7.6 %scatter_fusion.8 = f32[2048,512]{1,0:T(8,128)} fusion(f32[2048,512]{1,0:T(8,128)} %scatter_fusion.7, s32[512]{0:T(512)S(1)} %bitcast.70, f32[512,512]{1,0:T(8,128)S(1)} %convolution_divide_fusion), kind=kCustom, calls=%fused_computation.21 | custom fusion | flops 262144 | bytes 3147776 | tf_op jit(solution)/shard_map/scatter-add | solution.py:38
  102.7 2.5 convert.5
  105.2 0.8 slice.159
  106.0 1.0 slice.160
  107.1 0.1 reshape_squeeze.3
  107.2 0.6 gather_fusion
  107.9 0.1 slice_reduce_fusion.9
  108.0 54.8 %all-gather = bf16[512,512]{1,0:T(8,128)(2,1)} all-gather(bf16[16,512]{1,0:T(8,128)(2,1)S(1)} %gather_fusion), channel_id=2, replica_groups=mesh['dp'=8,'graph'=32] {'graph'}, dimensions={0}, use_global_device_ids=true | all-gather | bytes 540672 | tf_op jit(solution)/shard_map/all_gather | solution.py:16
  162.8 8.5 %all-to-all-start.1 = ((bf16[32,32,512]{2,1,0:T(8,128)(2,1)}), bf16[32,32,512]{2,1,0:T(8,128)(2,1)}, u32[]{:S(2)}, u32[]{:S(2)}) async-start(bf16[32,32,512]{2,1,0:T(8,128)(2,1)} %bitcast.67), calls=%async_computation.2 | async-start | bytes 2097152 | tf_op jit(solution)/shard_map/all_to_all | solution.py:42
  171.3 0.3 all-reduce.3.cloned.1.call-start
  171.5 1.5 fusion.8
  173.0 1.5 pad_maximum_fusion
  174.5 2.6 gather_fusion.10
  177.1 2.6 gather_fusion.11
  179.8 2.6 gather_fusion.2
  182.4 2.6 gather_fusion.3
  185.0 2.6 gather_fusion.4
  187.6 2.6 gather_fusion.5
  190.3 2.6 gather_fusion.6
  192.9 2.6 gather_fusion.7
  195.5 2.6 gather_fusion.8
  198.2 2.6 gather_fusion.9
  200.8 4.1 divide_convert_fusion
  204.9 1.4 fusion.6
  206.4 1.4 fusion.16
  207.8 1.8 convolution_add_fusion
  209.6 116.8 %reduce-scatter.2.cloned.1.call-done = bf16[16,512]{1,0:T(8,128)(2,1)} async-done(((bf16[512,512]{1,0:T(8,128)(2,1)}), bf16[16,512]{1,0:T(8,128)(2,1)}) %reduce-scatter.2.cloned.1.call-update) | async-done | bytes 16400 | tf_op jit(solution)/shard_map/reduce_scatter | solution.py:39
  326.3 1.3 scatter_custom_fusion.10
  327.6 7.9 %scatter_custom_fusion.11 = f32[512,512]{1,0:T(8,128)S(1)} fusion(f32[512,512]{1,0:T(8,128)S(1)} %scatter_custom_fusion.10, s32[1024]{0:T(1024)S(1)} %bitcast.91, bf16[1024,512]{1,0:T(8,128)(2,1)} %bitcast.33), kind=kCustom, calls=%fused_computation.25 | custom fusion | flops 1048576 | bytes 2097152 | tf_op jit(solution)/shard_map/scatter-add | solution.py:56
  335.5 2.5 fusion.5
  338.0 0.9 convert_bitcast_fusion
  338.9 133.6 %all-reduce.3.cloned.1.call-done = (f32[512,512]{1,0:T(8,128)}, f32[512,512]{1,0:T(8,128)}) async-done(((f32[512,512]{1,0:T(8,128)}, f32[512,512]{1,0:T(8,128)}), (f32[512,512]{1,0:T(8,128)}, f32[512,512]{1,0:T(8,128)})) %all-reduce.3.cloned.1.call-update) | async-done | bytes 2097168 | tf_op jit(solution)/shard_map/psum | solution.py:59
  472.4 1.4 dynamic-slice_multiply_fusion
  (41 shorter events, 0.3 us)
Async XLA Ops:
  8.0 19.0 %copy-start = (bf16[1,512,512]{2,1,0:T(8,128)(2,1)S(1)}, bf16[1,512,512]{2,1,0:T(8,128)(2,1)}, u32[]{:S(2)}) copy-start(bf16[1,512,512]{2,1,0:T(8,128)(2,1)} %param.9) | copy-start | bytes 1572868
  8.9 18.0 %copy-start.7 = (s32[1,512]{1,0:T(1,128)S(1)}, s32[1,512]{1,0:T(1,128)}, u32[]{:S(2)}) copy-start(s32[1,512]{1,0:T(1,128)} %param.13) | copy-start | bytes 6148
  8.9 18.0 %copy-start.6 = (s32[1,512,10]{1,0,2:T(1,128)S(1)}, s32[1,512,10]{1,0,2:T(1,128)}, u32[]{:S(2)}) copy-start(s32[1,512,10]{1,0,2:T(1,128)} %param.12) | copy-start | bytes 61444
  8.9 18.1 %copy-start.3 = (bf16[512,512]{1,0:T(8,128)(2,1)S(1)}, bf16[512,512]{1,0:T(8,128)(2,1)}, u32[]{:S(2)}) copy-start(bf16[512,512]{1,0:T(8,128)(2,1)} %param.11) | copy-start | bytes 1572868
  15.2 147.6 %all-to-all-start = ((bf16[32,32,512]{2,1,0:T(8,128)(2,1)}), bf16[32,32,512]{2,1,0:T(8,128)(2,1)}, u32[]{:S(2)}, u32[]{:S(2)}) async-start(bf16[32,32,512]{2,1,0:T(8,128)(2,1)} %bitcast.5), calls=%async_computation | async-start | bytes 2097152 | tf_op jit(solution)/shard_map/all_to_all | solution.py:18
  26.8 299.6 %reduce-scatter.2.cloned.1.call-start = ((), (), s32[]{:S(2)}) async-start(), calls=%async_computation.3 | async-start | bytes 540672 | tf_op jit(solution)/shard_map/reduce_scatter | solution.py:39
  102.6 4.4 copy-start.5
  102.6 4.5 copy-start.8
  102.7 4.5 copy-start.1
  162.8 164.8 %all-to-all-start.1 = ((bf16[32,32,512]{2,1,0:T(8,128)(2,1)}), bf16[32,32,512]{2,1,0:T(8,128)(2,1)}, u32[]{:S(2)}, u32[]{:S(2)}) async-start(bf16[32,32,512]{2,1,0:T(8,128)(2,1)} %bitcast.67), calls=%async_computation.2 | async-start | bytes 2097152 | tf_op jit(solution)/shard_map/all_to_all | solution.py:42
  171.3 301.2 %all-reduce.3.cloned.1.call-start = ((), (), s32[]{:S(2)}) async-start(), calls=%async_computation.4 | async-start | bytes 4194304 | tf_op jit(solution)/shard_map/psum | solution.py:59
  200.8 5.6 %copy-start.2 = (bf16[512,512]{1,0:T(8,128)(2,1)S(1)}, bf16[512,512]{1,0:T(8,128)(2,1)}, u32[]{:S(2)}) copy-start(bf16[512,512]{1,0:T(8,128)(2,1)} %param.10) | copy-start | bytes 1572868
  207.8 127.7 %copy-start.4 = (bf16[512,512]{1,0:T(8,128)(2,1)S(1)}, bf16[512,512]{1,0:T(8,128)(2,1)}, u32[]{:S(2)}) copy-start(bf16[512,512]{1,0:T(8,128)(2,1)} %param.11) | copy-start | bytes 1572868
Sparse Core Ops, SparseCore 0:
  106.1 220.1 reduce-scatter.1
Sparse Core Ops, SparseCore 1:
  206.4 265.9 all-reduce.2
where the time goes:
time: 490 us; the launch traced here: 482 us
  waiting for transfers between devices  250 us (51%)
  other arithmetic  95.6 us (20%)
  blocking collectives  54.8 us (11%)
  local copies, waits for them, and re-layouts  35.2 us (7%)
  starting transfers between devices  20.4 us (4%)
  between operations  16.1 us (3%)
  matrix products  9.02 us (2%)
    psum x1, waiting for transfers between devices, shards(): sum_self, sum_neigh = lax.psum((dws, dwn), ('dp', 'graph'))  134 us
    reduce_scatter x1, waiting for transfers between devices, shards(): lax.psum_scatter(dtable[rows:rows + nhub].astype(jnp.bfloat16), 'graph',...  117 us
    scatter-add x10, other arithmetic, shards(): dtable = dtable.at[target].add(back, mode='drop')  75.1 us
    all_gather x1, blocking collectives, shards(): hubs = lax.all_gather(hub_local, 'graph', axis=0, tiled=True)  54.8 us
    gather x10, local copies, waits for them, and re-layouts, shards(): table[idx[:, k]].astype(jnp.float32)  26.2 us
    all_to_all x1, starting transfers between devices, shards(): lax.all_to_all(outgoing, 'graph', split_axis=0, concat_axis=0, tiled=True)  11.6 us
  transfers between devices with their start and end apart: 4, of which 2 were waited for; matrix products, arithmetic and copies ran while one was open for 27% of the time, Pallas kernels for 0%

commit v1 on v0

--- a/solution.py
+++ b/solution.py
@@ -5,6 +5,18 @@
 
 
 def shards(feats, grad_out, w_self, w_neigh, nbr, deg, hub_rows, send_rows):
+
+    def view_the_blocks(mine_x, row_axis):
+        return jnp.concatenate(
+            lax.all_to_all(
+                jnp.stack([mine_x] * lax.axis_size(row_axis)),
+                axis_name=row_axis,
+                split_axis=0,
+                concat_axis=0,
+            ),
+            axis=0,
+        )
+
     own = feats[0]
     grads = grad_out[0]
     rows, width = own.shape
@@ -13,7 +25,7 @@
     hub_idx = hub_rows[0]
     sent_idx = send_rows[0, 0]
     hub_local = own[hub_idx]
-    hubs = lax.all_gather(hub_local, "graph", axis=0, tiled=True)
+    hubs = view_the_blocks(hub_local, row_axis="graph")
     outgoing = own[sent_idx]
     incoming = lax.all_to_all(outgoing, "graph", split_axis=0, concat_axis=0, tiled=True)
     nhub = hubs.shape[0]

time: 490 us -> 457 us (0.933)
  blocking collectives: 54.8 us -> 0 us
  waiting for transfers between devices: 250 us -> 262 us
  starting transfers between devices: 20.4 us -> 26.4 us
    all_gather x1 -> x0, blocking collectives: 54.8 us -> none  [shards(): hubs = lax.all_gather(hub_local, 'graph', axis=0, tiled=True)]
    reduce_scatter x1, waiting for transfers between devices: 117 us -> 170 us  [shards(): lax.psum_scatter(dtable[rows:rows + nhub].astype(jnp.bfloat16), 'graph',...]
    psum x1, waiting for transfers between devices: 134 us -> 82.1 us  [shards(): sum_self, sum_neigh = lax.psum((dws, dwn), ('dp', 'graph'))]
    all_to_all x0 -> x1, starting transfers between devices: none -> 11.5 us  [view_the_blocks(): lax.all_to_all(jnp.stack([mine_x] * lax.axis_size(row_axis)), axis_name=r...]
    all_to_all x0 -> x1, waiting for transfers between devices: none -> 10.4 us  [view_the_blocks(): lax.all_to_all(jnp.stack([mine_x] * lax.axis_size(row_axis)), axis_name=r...]
    all_to_all x1, starting transfers between devices: 11.6 us -> 4.77 us  [shards(): lax.all_to_all(outgoing, 'graph', split_axis=0, concat_axis=0, tiled=True)]
  transfers between devices with their start and end apart: 4 -> 5, of which waited for: 2 -> 3; matrix products, arithmetic and copies ran while one was open for 27% -> 31% of each run, Pallas kernels for 0% -> 0%
where the time goes in v1:
time: 457 us; the launch traced here: 448 us
  waiting for transfers between devices  262 us (57%)
  other arithmetic  97 us (21%)
  local copies, waits for them, and re-layouts  36.7 us (8%)
  starting transfers between devices  26.4 us (6%)
  between operations  16 us (4%)
  matrix products  9.02 us (2%)
    reduce_scatter x1, waiting for transfers between devices, shards(): lax.psum_scatter(dtable[rows:rows + nhub].astype(jnp.bfloat16), 'graph',...  170 us
    psum x1, waiting for transfers between devices, shards(): sum_self, sum_neigh = lax.psum((dws, dwn), ('dp', 'graph'))  82.1 us
    scatter-add x10, other arithmetic, shards(): dtable = dtable.at[target].add(back, mode='drop')  75.1 us
    gather x10, local copies, waits for them, and re-layouts, shards(): table[idx[:, k]].astype(jnp.float32)  26.2 us
    all_to_all x1, starting transfers between devices, view_the_blocks(): lax.all_to_all(jnp.stack([mine_x] * lax.axis_size(row_axis)), axis_name=r...  11.5 us
    all_to_all x1, waiting for transfers between devices, view_the_blocks(): lax.all_to_all(jnp.stack([mine_x] * lax.axis_size(row_axis)), axis_name=r...  10.4 us
    all_to_all x1, starting transfers between devices, shards(): lax.all_to_all(dtable[rows + nhub:].reshape(incoming.shape).astype(jnp.bf...  9.84 us
  transfers between devices with their start and end apart: 5, of which 3 were waited for; matrix products, arithmetic and copies ran while one was open for 31% of the time, Pallas kernels for 0%

profile of v1, /device:TPU:2, one launch (start us, length us, event | category | flops | bytes accessed | tf_op | source)
XLA Modules:
  0.0 447.6 jit_solution(8109289335680114093)
XLA Ops:
  8.0 0.7 fusion.14
  8.8 1.7 gather_fusion
  10.5 0.9 stack.2
  11.3 11.5 %all-to-all-start = ((bf16[32,16,512]{2,1,0:T(8,128)(2,1)}), bf16[32,16,512]{2,1,0:T(8,128)(2,1)S(1)}, u32[]{:S(2)}, u32[]{:S(2)}) async-start(bf16[32,16,512]{2,1,0:T(8,128)(2,1)} %stack.2), calls=%async_computation | async-start | bytes 1048576 | tf_op jit(solution)/shard_map/all_to_all | solution.py:11
  22.8 0.7 copy.14
  23.6 0.7 convert_element_type.65
  24.2 0.7 compare_select_fusion
  25.1 5.1 %gather_fusion.1 = bf16[1024,512]{1,0:T(8,128)(2,1)} fusion(bf16[512,512]{1,0:T(8,128)(2,1)S(1)} %bitcast.66, s32[1024]{0:T(1024)S(1)} %broadcast_clamp_fusion), kind=kCustom, calls=%fused_computation.1 | custom fusion | bytes 2101248 | tf_op jit(solution)/shard_map/gather | solution.py:29
  30.1 10.4 %all-to-all-done = bf16[32,16,512]{2,1,0:T(8,128)(2,1)S(1)} async-done(((bf16[32,16,512]{2,1,0:T(8,128)(2,1)}), bf16[32,16,512]{2,1,0:T(8,128)(2,1)S(1)}, u32[]{:S(2)}, u32[]{:S(2)}) %all-to-all-start) | async-done | bytes 524320 | tf_op jit(solution)/shard_map/all_to_all | solution.py:11
  40.6 4.8 %all-to-all-start.1 = ((bf16[32,32,512]{2,1,0:T(8,128)(2,1)}), bf16[32,32,512]{2,1,0:T(8,128)(2,1)}, u32[]{:S(2)}, u32[]{:S(2)}) async-start(bf16[32,32,512]{2,1,0:T(8,128)(2,1)} %bitcast.6), calls=%async_computation.1 | async-start | bytes 2097152 | tf_op jit(solution)/shard_map/all_to_all | solution.py:30
  45.5 0.5 convolution_divide_fusion
  46.0 5.7 %scatter_custom_fusion = f32[2048,512]{1,0:T(8,128)} fusion(s32[512]{0:T(512)S(1)} %bitcast.94, f32[512,512]{1,0:T(8,128)S(1)} %convolution_divide_fusion, f32[]{:T(128)} %constant.10.clone.1), kind=kCustom, calls=%fused_computation.27 | custom fusion | flops 262144 | bytes 4194308 | tf_op jit(solution)/shard_map/scatter-add | solution.py:50
  51.7 7.6 %scatter_fusion = f32[2048,512]{1,0:T(8,128)} fusion(f32[2048,512]{1,0:T(8,128)} %scatter_custom_fusion, s32[512]{0:T(512)S(1)} %bitcast.79, f32[512,512]{1,0:T(8,128)S(1)} %convolution_divide_fusion), kind=kCustom, calls=%fused_computation.13 | custom fusion | flops 262144 | bytes 3147776 | tf_op jit(solution)/shard_map/scatter-add | solution.py:50
  59.3 8.1 %scatter_fusion.1 = f32[2048,512]{1,0:T(8,128)} fusion(f32[2048,512]{1,0:T(8,128)} %scatter_fusion, s32[512]{0:T(512)S(1)} %bitcast.78, f32[512,512]{1,0:T(8,128)S(1)} %convolution_divide_fusion), kind=kCustom, calls=%fused_computation.14 | custom fusion | flops 262144 | bytes 3147776 | tf_op jit(solution)/shard_map/scatter-add | solution.py:50
  67.5 7.6 %scatter_fusion.2 = f32[2048,512]{1,0:T(8,128)} fusion(f32[2048,512]{1,0:T(8,128)} %scatter_fusion.1, s32[512]{0:T(512)S(1)} %bitcast.77, f32[512,512]{1,0:T(8,128)S(1)} %convolution_divide_fusion), kind=kCustom, calls=%fused_computation.15 | custom fusion | flops 262144 | bytes 3147776 | tf_op jit(solution)/shard_map/scatter-add | solution.py:50
  75.1 7.6 %scatter_fusion.3 = f32[2048,512]{1,0:T(8,128)} fusion(f32[2048,512]{1,0:T(8,128)} %scatter_fusion.2, s32[512]{0:T(512)S(1)} %bitcast.76, f32[512,512]{1,0:T(8,128)S(1)} %convolution_divide_fusion), kind=kCustom, calls=%fused_computation.16 | custom fusion | flops 262144 | bytes 3147776 | tf_op jit(solution)/shard_map/scatter-add | solution.py:50
  82.8 7.6 %scatter_fusion.4 = f32[2048,512]{1,0:T(8,128)} fusion(f32[2048,512]{1,0:T(8,128)} %scatter_fusion.3, s32[512]{0:T(512)S(1)} %bitcast.75, f32[512,512]{1,0:T(8,128)S(1)} %convolution_divide_fusion), kind=kCustom, calls=%fused_computation.17 | custom fusion | flops 262144 | bytes 3147776 | tf_op jit(solution)/shard_map/scatter-add | solution.py:50
  90.4 7.8 %scatter_fusion.5 = f32[2048,512]{1,0:T(8,128)} fusion(f32[2048,512]{1,0:T(8,128)} %scatter_fusion.4, s32[512]{0:T(512)S(1)} %bitcast.74, f32[512,512]{1,0:T(8,128)S(1)} %convolution_divide_fusion), kind=kCustom, calls=%fused_computation.18 | custom fusion | flops 262144 | bytes 3147776 | tf_op jit(solution)/shard_map/scatter-add | solution.py:50
  98.2 7.6 %scatter_fusion.6 = f32[2048,512]{1,0:T(8,128)} fusion(f32[2048,512]{1,0:T(8,128)} %scatter_fusion.5, s32[512]{0:T(512)S(1)} %bitcast.73, f32[512,512]{1,0:T(8,128)S(1)} %convolution_divide_fusion), kind=kCustom, calls=%fused_computation.19 | custom fusion | flops 262144 | bytes 3147776 | tf_op jit(solution)/shard_map/scatter-add | solution.py:50
  105.9 7.6 %scatter_fusion.7 = f32[2048,512]{1,0:T(8,128)} fusion(f32[2048,512]{1,0:T(8,128)} %scatter_fusion.6, s32[512]{0:T(512)S(1)} %bitcast.80, f32[512,512]{1,0:T(8,128)S(1)} %convolution_divide_fusion), kind=kCustom, calls=%fused_computation.20 | custom fusion | flops 262144 | bytes 3147776 | tf_op jit(solution)/shard_map/scatter-add | solution.py:50
  113.5 7.6 %scatter_fusion.8 = f32[2048,512]{1,0:T(8,128)} fusion(f32[2048,512]{1,0:T(8,128)} %scatter_fusion.7, s32[512]{0:T(512)S(1)} %bitcast.72, f32[512,512]{1,0:T(8,128)S(1)} %convolution_divide_fusion), kind=kCustom, calls=%fused_computation.21 | custom fusion | flops 262144 | bytes 3147776 | tf_op jit(solution)/shard_map/scatter-add | solution.py:50
  121.2 2.5 convert.5
  123.6 0.8 slice.159
  124.5 1.0 slice.160
  125.8 9.8 %all-to-all-start.2 = ((bf16[32,32,512]{2,1,0:T(8,128)(2,1)}), bf16[32,32,512]{2,1,0:T(8,128)(2,1)}, u32[]{:S(2)}, u32[]{:S(2)}) async-start(bf16[32,32,512]{2,1,0:T(8,128)(2,1)} %bitcast.68), calls=%async_computation.3 | async-start | bytes 2097152 | tf_op jit(solution)/shard_map/all_to_all | solution.py:54
  136.0 1.5 fusion.8
  137.4 1.5 pad_maximum_fusion
  138.9 2.6 gather_fusion.10
  141.6 2.6 gather_fusion.11
  144.2 2.6 gather_fusion.2
  146.8 2.6 gather_fusion.3
  149.4 2.6 gather_fusion.4
  152.1 2.6 gather_fusion.5
  154.7 2.6 gather_fusion.6
  157.3 2.6 gather_fusion.7
  160.0 2.6 gather_fusion.8
  162.6 2.6 gather_fusion.9
  165.2 4.1 divide_convert_fusion
  169.3 1.4 fusion.6
  170.8 1.4 fusion.16
  172.2 1.8 convolution_add_fusion
  174.0 169.8 %reduce-scatter.2.cloned.1.call-done = bf16[16,512]{1,0:T(8,128)(2,1)} async-done(((bf16[512,512]{1,0:T(8,128)(2,1)}), bf16[16,512]{1,0:T(8,128)(2,1)}) %reduce-scatter.2.cloned.1.call-update) | async-done | bytes 16400 | tf_op jit(solution)/shard_map/reduce_scatter | solution.py:51
  343.8 1.3 scatter_custom_fusion.10
  345.1 7.9 %scatter_custom_fusion.11 = f32[512,512]{1,0:T(8,128)S(1)} fusion(f32[512,512]{1,0:T(8,128)S(1)} %scatter_custom_fusion.10, s32[1024]{0:T(1024)S(1)} %bitcast.93, bf16[1024,512]{1,0:T(8,128)(2,1)} %bitcast.34), kind=kCustom, calls=%fused_computation.25 | custom fusion | flops 1048576 | bytes 2097152 | tf_op jit(solution)/shard_map/scatter-add | solution.py:68
  353.0 2.5 fusion.5
  355.5 0.9 convert_bitcast_fusion
  356.3 82.1 %all-reduce.3.cloned.1.call-done = (f32[512,512]{1,0:T(8,128)}, f32[512,512]{1,0:T(8,128)}) async-done(((f32[512,512]{1,0:T(8,128)}, f32[512,512]{1,0:T(8,128)}), (f32[512,512]{1,0:T(8,128)}, f32[512,512]{1,0:T(8,128)})) %all-reduce.3.cloned.1.call-update) | async-done | bytes 2097168 | tf_op jit(solution)/shard_map/psum | solution.py:71
  438.5 1.4 dynamic-slice_multiply_fusion
  (41 shorter events, 0.8 us)
Async XLA Ops:
  8.0 37.5 %copy-start = (bf16[1,512,512]{2,1,0:T(8,128)(2,1)S(1)}, bf16[1,512,512]{2,1,0:T(8,128)(2,1)}, u32[]{:S(2)}) copy-start(bf16[1,512,512]{2,1,0:T(8,128)(2,1)} %param.9) | copy-start | bytes 1572868
  8.0 17.0 %copy-start.1 = (bf16[1,512,512]{2,1,0:T(8,128)(2,1)S(1)}, bf16[1,512,512]{2,1,0:T(8,128)(2,1)}, u32[]{:S(2)}) copy-start(bf16[1,512,512]{2,1,0:T(8,128)(2,1)} %param.8) | copy-start | bytes 1572868
  11.3 29.3 %all-to-all-start = ((bf16[32,16,512]{2,1,0:T(8,128)(2,1)}), bf16[32,16,512]{2,1,0:T(8,128)(2,1)S(1)}, u32[]{:S(2)}, u32[]{:S(2)}) async-start(bf16[32,16,512]{2,1,0:T(8,128)(2,1)} %stack.2), calls=%async_computation | async-start | bytes 1048576 | tf_op jit(solution)/shard_map/all_to_all | solution.py:11
  25.0 5.1 %copy-start.7 = (s32[1,512]{1,0:T(1,128)S(1)}, s32[1,512]{1,0:T(1,128)}, u32[]{:S(2)}) copy-start(s32[1,512]{1,0:T(1,128)} %param.13) | copy-start | bytes 6148
  25.1 20.4 %copy-start.4 = (bf16[512,512]{1,0:T(8,128)(2,1)S(1)}, bf16[512,512]{1,0:T(8,128)(2,1)}, u32[]{:S(2)}) copy-start(bf16[512,512]{1,0:T(8,128)(2,1)} %param.11) | copy-start | bytes 1572868
  40.6 4.8 %copy-start.3 = (bf16[32,16,512]{2,1,0:T(8,128)(2,1)}, bf16[32,16,512]{2,1,0:T(8,128)(2,1)S(1)}, u32[]{:S(2)}) copy-start(bf16[32,16,512]{2,1,0:T(8,128)(2,1)S(1)} %all-to-all-done) | copy-start | bytes 1572868
  40.6 85.2 %all-to-all-start.1 = ((bf16[32,32,512]{2,1,0:T(8,128)(2,1)}), bf16[32,32,512]{2,1,0:T(8,128)(2,1)}, u32[]{:S(2)}, u32[]{:S(2)}) async-start(bf16[32,32,512]{2,1,0:T(8,128)(2,1)} %bitcast.6), calls=%async_computation.1 | async-start | bytes 2097152 | tf_op jit(solution)/shard_map/all_to_all | solution.py:30
  45.4 298.5 %reduce-scatter.2.cloned.1.call-start = ((), (), s32[]{:S(2)}) async-start(), calls=%async_computation.4 | async-start | bytes 540672 | tf_op jit(solution)/shard_map/reduce_scatter | solution.py:51
  121.2 4.4 copy-start.6
  125.8 219.3 %all-to-all-start.2 = ((bf16[32,32,512]{2,1,0:T(8,128)(2,1)}), bf16[32,32,512]{2,1,0:T(8,128)(2,1)}, u32[]{:S(2)}, u32[]{:S(2)}) async-start(bf16[32,32,512]{2,1,0:T(8,128)(2,1)} %bitcast.68), calls=%async_computation.3 | async-start | bytes 2097152 | tf_op jit(solution)/shard_map/all_to_all | solution.py:54
  135.7 302.8 %all-reduce.3.cloned.1.call-start = ((), (), s32[]{:S(2)}) async-start(), calls=%async_computation.5 | async-start | bytes 4194304 | tf_op jit(solution)/shard_map/psum | solution.py:71
  165.2 5.6 %copy-start.2 = (bf16[512,512]{1,0:T(8,128)(2,1)S(1)}, bf16[512,512]{1,0:T(8,128)(2,1)}, u32[]{:S(2)}) copy-start(bf16[512,512]{1,0:T(8,128)(2,1)} %param.10) | copy-start | bytes 1572868
  172.2 180.8 %copy-start.5 = (bf16[512,512]{1,0:T(8,128)(2,1)S(1)}, bf16[512,512]{1,0:T(8,128)(2,1)}, u32[]{:S(2)}) copy-start(bf16[512,512]{1,0:T(8,128)(2,1)} %param.11) | copy-start | bytes 1572868
Sparse Core Ops, SparseCore 0:
  124.6 219.1 reduce-scatter.1
Sparse Core Ops, SparseCore 1:
  170.9 267.5 all-reduce.2
